TPU v7x, 128 devices: a whole 4x4x4 slice. The times are simulated.
128 devices in a mesh: pipe: 16 (over y_lo, z, core), seq: 8 (over x, y_hi).
Axes of the slice: x: 4, y: 4 (y_hi: 2, y_lo: 2; y = y_hi * 2 + y_lo), z: 4, core: 2. Of those that a mesh axis runs over, the one named last changes fastest.
Arguments:
- x_fwd: float32 [16, 1024, 2048], P('pipe', 'seq'), may hold values from -12 to 12
- x_bwd: float32 [16, 1024, 2048], P('pipe', 'seq'), may hold values from -12 to 12
- grad_in: float32 [16, 1024, 2048], P('pipe', 'seq'), may hold values from -6 to 6
- gain: float32 [16, 2048], P('pipe'), may hold values from 0.25 to 1.75
- w_query: bfloat16 [16, 2048, 2048], P('pipe', None, 'seq'), may hold values from -2 to 2
- w_key: bfloat16 [16, 2048, 2048], P('pipe', None, 'seq'), may hold values from -2 to 2
- w_value: bfloat16 [16, 2048, 2048], P('pipe', None, 'seq'), may hold values from -0.125 to 0.125
- w_out: bfloat16 [16, 2048, 2048], P('pipe', None, 'seq'), may hold values from -0.125 to 0.125
Outputs:
- act_next: float32 [16, 1024, 2048], P('pipe', 'seq')
- grad_prev: float32 [16, 1024, 2048], P('pipe', 'seq')
All inputs are finite; a program needn't handle non-finite values.
Results may differ from a plain program's by a relative error of at most 0.012.
The roundings to bfloat16 on the way count: a program that leaves them out, or rounds other values in their place, can miss the bound.
Values may be sent and summed in bfloat16 or wider, within the bound.
A program may use at most 192 MiB of HBM per device.

v0:
```python
import jax
import jax.numpy as jnp
from jax import lax
from jax.sharding import PartitionSpec as P

HD = 128


def passed_along(value, axis, steps):
    count = lax.axis_size(axis)
    pairs = [(source, (source + steps) % count) for source in range(count)]
    return lax.ppermute(value, axis, pairs)


def rope_tables(positions):
    half_dim = HD // 2
    inverse = 10000.0 ** (-(jnp.arange(half_dim).astype(jnp.float32) * 2.0 / HD))
    angles = positions.astype(jnp.float32)[:, None] * inverse[None, :]
    return (jnp.cos(angles)[:, None, :], jnp.sin(angles)[:, None, :])


def rotate(values, cosine, sine_table):
    shaped = values.reshape(values.shape[0], -1, HD)
    first_half = shaped[..., : HD // 2]
    second_half = shaped[..., HD // 2 :]
    output = jnp.concatenate(
        [
            first_half * cosine - second_half * sine_table,
            second_half * cosine + first_half * sine_table,
        ],
        -1,
    )
    return output.reshape(values.shape)


def rotate_back(values, cosine, sine_table):
    shaped = values.reshape(values.shape[0], -1, HD)
    first_half = shaped[..., : HD // 2]
    second_half = shaped[..., HD // 2 :]
    output = jnp.concatenate(
        [
            first_half * cosine + second_half * sine_table,
            second_half * cosine - first_half * sine_table,
        ],
        -1,
    )
    return output.reshape(values.shape)


def normalize(inputs, gain_row):
    inv_rms = lax.rsqrt(jnp.mean(inputs * inputs, -1, keepdims=True) + 1e-05)
    return ((inputs * inv_rms * gain_row).astype(jnp.bfloat16), inv_rms)


def times_t(left, right):
    return lax.dot_general(
        left, right, (((1,), (1,)), ((), ())), preferred_element_type=jnp.float32
    )


def split_heads(values):
    return values.reshape(values.shape[0], -1, HD)


def attend(query, key_rows, value_rows):
    length = query.shape[0]
    score_scale = HD ** (-0.5)
    key_heads = split_heads(key_rows)
    value_heads = split_heads(value_rows)
    query_blocks = split_heads(query).reshape(length // length, length, -1, HD)

    def one_block(query_block):
        scores = (
            jnp.einsum("qhd,khd->hqk", query_block, key_heads, preferred_element_type=jnp.float32)
            * score_scale
        )
        probs = jax.nn.softmax(scores, axis=-1)
        output = jnp.einsum(
            "hqk,khd->qhd",
            probs.astype(jnp.bfloat16),
            value_heads,
            preferred_element_type=jnp.float32,
        )
        return output.astype(jnp.bfloat16)

    return lax.map(one_block, query_blocks).reshape(length, -1)


def attend_back(query, key_rows, value_rows, grad_out, cosine, sine_table):
    length = query.shape[0]
    score_scale = HD ** (-0.5)
    key_heads = split_heads(key_rows)
    value_heads = split_heads(value_rows)
    query_blocks = split_heads(query).reshape(length // length, length, -1, HD)
    grad_blocks = split_heads(grad_out).reshape(length // length, length, -1, HD)

    def step(totals, operands):
        query_block, grad_block = operands
        scores = (
            jnp.einsum("qhd,khd->hqk", query_block, key_heads, preferred_element_type=jnp.float32)
            * score_scale
        )
        probs = jax.nn.softmax(scores, axis=-1)
        value_grad = jnp.einsum(
            "hqk,qhd->khd",
            probs.astype(jnp.bfloat16),
            grad_block,
            preferred_element_type=jnp.float32,
        )
        prob_grad = jnp.einsum(
            "qhd,khd->hqk", grad_block, value_heads, preferred_element_type=jnp.float32
        )
        row_delta = jnp.sum(probs * prob_grad, -1, keepdims=True)
        score_grad = (probs * (prob_grad - row_delta) * score_scale).astype(jnp.bfloat16)
        query_grad = jnp.einsum(
            "hqk,khd->qhd", score_grad, key_heads, preferred_element_type=jnp.float32
        )
        key_grad = jnp.einsum(
            "hqk,qhd->khd", score_grad, query_block, preferred_element_type=jnp.float32
        )
        return ((totals[0] + key_grad, totals[1] + value_grad), query_grad)

    zero_heads = jnp.zeros(key_heads.shape, jnp.float32)
    (key_total, value_total), query_grads = lax.scan(
        step, (zero_heads, zero_heads), (query_blocks, grad_blocks)
    )
    query_grad = rotate_back(query_grads.reshape(length, -1), cosine, sine_table).astype(
        jnp.bfloat16
    )
    key_grad = rotate_back(key_total.reshape(length, -1), cosine, sine_table).astype(jnp.bfloat16)
    return (query_grad, key_grad, value_total.reshape(length, -1).astype(jnp.bfloat16))


def to_tokens(values):
    return lax.all_to_all(values, "seq", split_axis=1, concat_axis=2, tiled=True)


def shards(x_fwd, x_bwd, grad_in, gain, w_query, w_key, w_value, w_out):
    act_in = x_fwd[0]
    saved_in = x_bwd[0]
    grad = grad_in[0]
    gain_row = gain[0]
    local_rows = act_in.shape[0]
    length = local_rows * lax.axis_size("seq")
    normed_fwd, inv_fwd = normalize(act_in, gain_row)
    normed_bwd, inv_bwd = normalize(saved_in, gain_row)
    grad_low = grad.astype(jnp.bfloat16)
    full_cos, full_sin = rope_tables(jnp.arange(length))
    all_query, all_key, all_value, all_out = (
        lax.all_gather(w_query[0], "seq", axis=1, tiled=True),
        lax.all_gather(w_key[0], "seq", axis=1, tiled=True),
        lax.all_gather(w_value[0], "seq", axis=1, tiled=True),
        lax.all_gather(w_out[0], "seq", axis=1, tiled=True),
    )
    local_cos, local_sin = rope_tables(lax.axis_index("seq") * local_rows + jnp.arange(local_rows))

    def project_local(normed):
        query = rotate(
            jnp.dot(normed, all_query, preferred_element_type=jnp.float32), local_cos, local_sin
        ).astype(jnp.bfloat16)
        key_rows = rotate(
            jnp.dot(normed, all_key, preferred_element_type=jnp.float32), local_cos, local_sin
        ).astype(jnp.bfloat16)
        value_rows = jnp.dot(normed, all_value, preferred_element_type=jnp.float32).astype(
            jnp.bfloat16
        )
        return [query, key_rows, value_rows]

    attn_grad = jnp.dot(grad_low, all_out, preferred_element_type=jnp.float32).astype(jnp.bfloat16)
    pieces = jnp.stack(project_local(normed_fwd) + project_local(normed_bwd) + [attn_grad])
    head_view = lax.all_to_all(pieces, "seq", split_axis=2, concat_axis=1, tiled=True)
    attn = attend(head_view[0], head_view[1], head_view[2])
    attn_tokens = to_tokens(attn[None])[0]
    branch = times_t(attn_tokens, all_out)
    query_grad, key_grad, value_grad = attend_back(
        head_view[3], head_view[4], head_view[5], head_view[6], full_cos, full_sin
    )
    grad_tokens = to_tokens(jnp.stack([query_grad, key_grad, value_grad]))
    d_normed = (
        times_t(grad_tokens[0], all_query)
        + times_t(grad_tokens[1], all_key)
        + times_t(grad_tokens[2], all_value)
    )
    act_out = act_in + branch
    gain_grad = d_normed * gain_row
    d_input = inv_bwd * gain_grad - saved_in * inv_bwd * inv_bwd * inv_bwd * jnp.mean(
        saved_in * gain_grad, -1, keepdims=True
    )
    sent_forward = passed_along(act_out.astype(jnp.bfloat16), "pipe", 1).astype(act_out.dtype)
    sent_backward = passed_along((grad + d_input).astype(jnp.bfloat16), "pipe", -1).astype(
        jnp.float32
    )
    return (sent_forward[None], sent_backward[None])


def solution(mesh):
    placed = (
        P("pipe", "seq", None),
        P("pipe", "seq", None),
        P("pipe", "seq", None),
        P("pipe", None),
        P("pipe", None, "seq"),
        P("pipe", None, "seq"),
        P("pipe", None, "seq"),
        P("pipe", None, "seq"),
    )
    return jax.shard_map(
        shards,
        mesh=mesh,
        in_specs=placed,
        out_specs=(P("pipe", "seq", None), P("pipe", "seq", None)),
        check_vma=False,
    )
```

profile of v0, /device:TPU:1, one launch (start us, length us, event | category | flops | bytes accessed | tf_op | source)
XLA Modules:
  0.0 765.0 jit_solution(12762140533666074192)
XLA Ops:
  13.0 118.5 %all-gather.11.cloned.1.call-done = bf16[1,2048,2048]{2,1,0:T(8,128)(2,1)} async-done(((bf16[1,2048,256]{2,1,0:T(8,128)(2,1)}), bf16[1,2048,2048]{2,1,0:T(8,128)(2,1)}) %all-gather.11.cloned.1.call-update) | async-done | bytes 8388624 | tf_op jit(solution)/shard_map/all_gather | solution.py:151
  131.5 12.4 %copy.67 = bf16[2048,2048]{1,0:T(8,128)(2,1)} copy(bf16[2048,2048]{0,1:T(8,128)(2,1)} %bitcast.212) | data formatting | bytes 16777216 | tf_op jit(solution)/shard_map/dot_general | solution.py:162
  143.8 108.1 %all-gather.9.cloned.1.call-done = bf16[1,2048,2048]{2,1,0:T(8,128)(2,1)} async-done(((bf16[1,2048,256]{2,1,0:T(8,128)(2,1)}), bf16[1,2048,2048]{2,1,0:T(8,128)(2,1)}) %all-gather.9.cloned.1.call-update) | async-done | bytes 8388624 | tf_op jit(solution)/shard_map/all_gather | solution.py:150
  251.9 12.4 %copy.66 = bf16[2048,2048]{1,0:T(8,128)(2,1)} copy(bf16[2048,2048]{0,1:T(8,128)(2,1)} %bitcast.213) | data formatting | bytes 16777216 | tf_op jit(solution)/shard_map/dot_general | solution.py:159
  264.3 6.5 fusion.112
  270.9 2.5 fusion.116
  273.6 2.5 fusion.114
  276.1 2.5 fusion.118
  282.4 2.2 pad_maximum_fusion.1
  292.4 80.0 %all-gather.13.cloned.1.call-done = bf16[1,2048,2048]{2,1,0:T(8,128)(2,1)} async-done(((bf16[1,2048,256]{2,1,0:T(8,128)(2,1)}), bf16[1,2048,2048]{2,1,0:T(8,128)(2,1)}) %all-gather.13.cloned.1.call-update) | async-done | bytes 8388624 | tf_op jit(solution)/shard_map/all_gather | solution.py:152
  372.5 5.6 fusion.76
  379.8 2.6 fusion.70
  382.4 110.4 %all-gather.15.cloned.1.call-done = bf16[1,2048,2048]{2,1,0:T(8,128)(2,1)} async-done(((bf16[1,2048,256]{2,1,0:T(8,128)(2,1)}), bf16[1,2048,2048]{2,1,0:T(8,128)(2,1)}) %all-gather.15.cloned.1.call-update) | async-done | bytes 8388624 | tf_op jit(solution)/shard_map/all_gather | solution.py:153
  492.8 5.4 fusion.64
  498.3 6.5 copy.72
  504.7 4.5 all-to-all-start
  511.1 56.6 %all-to-all-done = bf16[7,128,2048]{1,0,2:T(8,128)(2,1)} async-done(((bf16[7,128,2048]{1,0,2:T(8,128)(2,1)}), bf16[7,128,2048]{1,0,2:T(8,128)(2,1)}, u32[]{:S(2)}, u32[]{:S(2)}) %all-to-all-start) | async-done | bytes 3670048 | tf_op jit(solution)/shard_map/all_to_all | solution.py:171
  567.7 4.8 copy.105
  574.4 2.1 reshape_squeeze.15
  580.6 2.1 reshape_squeeze.14
  582.7 5.7 fusion.127
  588.4 7.2 fusion.124
  595.6 5.9 fusion.86
  601.5 14.8 %fusion.82 = f32[1024,2,128]{0,2,1:T(8,128)} fusion(bf16[1024,2,128]{0,2,1:T(8,128)(2,1)} %squeeze.55, f32[2,1024,1024]{1,2,0:T(8,128)} %fusion.127, f32[2,1024,1024]{1,2,0:T(8,128)} %get-tuple-element.78, f32[2,1024]{1,0:T(2,128)S(1)} %get-tuple-element.77), kind=kOutput, calls=%fused_computation.52 | convolution fusion | flops 551554048 | bytes 18358272 | tf_op jit(solution)/shard_map/while/body/eval_jaxpr/hqk,qhd->khd/dot_general | solution.py:118
  616.2 14.8 %fusion.79 = f32[1024,2,128]{0,2,1:T(8,128)} fusion(bf16[1024,2,128]{0,2,1:T(8,128)(2,1)} %reshape_squeeze.14, f32[2,1024,1024]{1,2,0:T(8,128)} %fusion.127, f32[2,1024,1024]{1,2,0:T(8,128)} %get-tuple-element.78, f32[2,1024]{1,0:T(2,128)S(1)} %get-tuple-element.77), kind=kOutput, calls=%fused_computation.51 | convolution fusion | flops 551554048 | bytes 18358272 | tf_op jit(solution)/shard_map/while/body/eval_jaxpr/hqk,khd->qhd/dot_general | solution.py:115
  633.1 2.1 squeeze.53
  637.3 7.2 fusion.123
  644.5 5.1 fusion.85
  649.6 3.6 copy.77
  653.7 5.6 reduce
  661.3 4.4 all-to-all-start.1
  665.7 2.7 add_convert_fusion.1
  669.2 3.6 copy.88
  672.8 3.6 copy.86
  678.2 3.6 copy.87
  681.8 6.0 pad_maximum_fusion
  687.7 6.6 all-to-all-start.2
  694.4 3.5 reshape.322
  697.8 2.1 copy.103
  702.0 7.3 fusion.58
  709.2 4.0 collective-permute-start
  713.3 9.9 %all-to-all-done.2 = bf16[3,1024,256]{2,0,1:T(4,128)(2,1)} async-done(((bf16[3,1024,256]{2,0,1:T(4,128)(2,1)}), bf16[3,1024,256]{2,0,1:T(4,128)(2,1)}, u32[]{:S(2)}, u32[]{:S(2)}) %all-to-all-start.2) | async-done | bytes 1572896 | tf_op jit(solution)/shard_map/all_to_all | solution.py:135
  730.0 6.6 fusion.13
  736.6 6.5 fusion.37
  743.1 3.0 fusion.91
  746.4 2.4 collective-permute-start.1
  748.9 2.1 bitcast_convert_fusion.3
  751.0 5.9 collective-permute-done.1
  (73 shorter events, 46.9 us)
Async XLA Ops:
  7.2 124.3 %all-gather.11.cloned.1.call-start = ((), (), s32[]{:S(2)}) async-start(), calls=%async_computation.4 | async-start | bytes 9437184 | tf_op jit(solution)/shard_map/all_gather | solution.py:151
  7.9 244.0 %all-gather.9.cloned.1.call-start = ((), (), s32[]{:S(2)}) async-start(), calls=%async_computation.3 | async-start | bytes 9437184 | tf_op jit(solution)/shard_map/all_gather | solution.py:150
  8.6 363.8 %all-gather.13.cloned.1.call-start = ((), (), s32[]{:S(2)}) async-start(), calls=%async_computation.5 | async-start | bytes 9437184 | tf_op jit(solution)/shard_map/all_gather | solution.py:152
  9.4 483.4 %all-gather.15.cloned.1.call-start = ((), (), s32[]{:S(2)}) async-start(), calls=%async_computation.6 | async-start | bytes 9437184 | tf_op jit(solution)/shard_map/all_gather | solution.py:153
  251.9 12.4 %copy-start.2 = (f32[1,128,2048]{2,1,0:T(8,128)S(1)}, f32[1,128,2048]{2,1,0:T(8,128)}, u32[]{:S(2)}) copy-start(f32[1,128,2048]{2,1,0:T(8,128)} %param.9) | copy-start | bytes 3145732
  251.9 12.4 %copy-start.7 = (f32[1,2048]{1,0:T(1,128)S(1)}, f32[1,2048]{1,0:T(1,128)}, u32[]{:S(2)}) copy-start(f32[1,2048]{1,0:T(1,128)} %param.11) | copy-start | bytes 24580
  264.3 6.5 copy-start.1
  264.3 6.6 copy-start.3
  264.3 9.1 %slice-start.2 = ((s8[8388608]{0:T(1024)(128)(4,1)}), s8[4194304]{0:T(1024)(128)(4,1)S(1)}, s32[]{:S(2)}) async-start(s8[8388608]{0:T(1024)(128)(4,1)} %bitcast.208), calls=%async_computation.9 | async-start | bytes 8388608
  270.9 2.7 slice-start.3
  372.5 7.3 copy-start
  379.8 113.0 %copy-start.4 = (f32[1,128,2048]{2,1,0:T(8,128)S(1)}, f32[1,128,2048]{2,1,0:T(8,128)}, u32[]{:S(2)}) copy-start(f32[1,128,2048]{2,1,0:T(8,128)} %param.10) | copy-start | bytes 3145732
  504.7 62.9 %all-to-all-start = ((bf16[7,128,2048]{1,0,2:T(8,128)(2,1)}), bf16[7,128,2048]{1,0,2:T(8,128)(2,1)}, u32[]{:S(2)}, u32[]{:S(2)}) async-start(bf16[7,128,2048]{1,0,2:T(8,128)(2,1)} %copy.72), calls=%async_computation | async-start | bytes 8388608 | tf_op jit(solution)/shard_map/all_to_all | solution.py:171
  661.3 26.4 %all-to-all-start.1 = ((bf16[8,2,16384]{2,1,0:T(2,128)(2,1)}), bf16[8,2,16384]{2,1,0:T(2,128)(2,1)}, u32[]{:S(2)}, u32[]{:S(2)}) async-start(bf16[8,2,16384]{2,1,0:T(2,128)(2,1)} %reshape.321), calls=%async_computation.1 | async-start | bytes 1048576 | tf_op jit(solution)/shard_map/all_to_all | solution.py:135
  687.7 35.4 %all-to-all-start.2 = ((bf16[3,1024,256]{2,0,1:T(4,128)(2,1)}), bf16[3,1024,256]{2,0,1:T(4,128)(2,1)}, u32[]{:S(2)}, u32[]{:S(2)}) async-start(bf16[3,1024,256]{2,0,1:T(4,128)(2,1)} %pad_maximum_fusion), calls=%async_computation.2 | async-start | bytes 4194304 | tf_op jit(solution)/shard_map/all_to_all | solution.py:135
  709.2 39.6 %collective-permute-start = (bf16[128,2048]{1,0:T(8,128)(2,1)}, bf16[128,2048]{1,0:T(8,128)(2,1)}, u32[]{:S(2)}, u32[]{:S(2)}) collective-permute-start(bf16[128,2048]{1,0:T(8,128)(2,1)} %fusion.58), channel_id=1, source_target_pairs={{0,8},{8,16},{16,24},{24,32},{32,40},{40,48},{48,56},{56,64},{64,7... | collective-permute-start | bytes 1572872 | tf_op jit(solution)/shard_map/ppermute | solution.py:12
  729.9 6.6 copy-start.6
  729.9 13.1 %slice-start = ((s8[8388608]{0:T(1024)(128)(4,1)}), s8[4194304]{0:T(1024)(128)(4,1)S(1)}, s32[]{:S(2)}) async-start(s8[8388608]{0:T(1024)(128)(4,1)} %bitcast.204), calls=%async_computation.7 | async-start | bytes 8388608
  730.0 13.1 %copy-start.5 = (bf16[1,128,8,256]{1,3,2,0:T(8,128)(2,1)S(1)}, bf16[1,128,8,256]{1,3,2,0:T(8,128)(2,1)}, u32[]{:S(2)}) copy-start(bf16[1,128,8,256]{1,3,2,0:T(8,128)(2,1)} %copy.92) | copy-start | bytes 1572868
  736.6 6.5 slice-start.1
  746.4 10.5 %collective-permute-start.1 = (bf16[128,2048]{1,0:T(8,128)(2,1)S(1)}, bf16[128,2048]{1,0:T(8,128)(2,1)S(1)}, u32[]{:S(2)}, u32[]{:S(2)}) collective-permute-start(bf16[128,2048]{1,0:T(8,128)(2,1)S(1)} %fusion.89), channel_id=1, source_target_pairs={{0,120},{8,0},{16,8},{24,16},{32,24},{40,32},{48,40},{56,48},{64,5... | collective-permute-start | bytes 1572872 | tf_op jit(solution)/shard_map/ppermute | solution.py:12
Sparse Core Ops, SparseCore 0:
  10.2 121.2 all-gather.10
  133.6 118.2 all-gather.8
  254.1 118.3 all-gather.12
  374.5 118.2 all-gather.14
where the time goes:
time: 777 us; the launch traced here: 765 us
  waiting for transfers between devices  492 us (63%)
  matrix products  112 us (14%)
  local copies, waits for them, and re-layouts  95 us (12%)
  other arithmetic  29.8 us (4%)
  starting transfers between devices  22.1 us (3%)
  between operations  14.4 us (2%)
    all_gather x1, waiting for transfers between devices, shards(): lax.all_gather(w_key[0], 'seq', axis=1, tiled=True)  118 us
    all_gather x1, waiting for transfers between devices, shards(): lax.all_gather(w_out[0], 'seq', axis=1, tiled=True)  110 us
    all_gather x1, waiting for transfers between devices, shards(): lax.all_gather(w_query[0], 'seq', axis=1, tiled=True)  108 us
    all_gather x1, waiting for transfers between devices, shards(): lax.all_gather(w_value[0], 'seq', axis=1, tiled=True)  80 us
    all_to_all x1, waiting for transfers between devices, shards(): lax.all_to_all(pieces, 'seq', split_axis=2, concat_axis=1, tiled=True)  56.6 us
    dot_general x4, matrix products, times_t(): lax.dot_general(left, right, (((1,), (1,)), ((), ())), preferred_element_...  23.4 us
  transfers between devices with their start and end apart: 9, of which 7 were waited for; matrix products, arithmetic and copies ran while one was open for 17% of the time, Pallas kernels for 0%

commit v1 on v0

--- a/solution.py
+++ b/solution.py
@@ -4,6 +4,13 @@
 from jax.sharding import PartitionSpec as P
 
 HD = 128
+
+
+def stacked_exchange(x, axis, split, join):
+    peers = lax.axis_size(axis)
+    pieces = jnp.stack(jnp.split(x, peers, axis=split), axis=0)
+    pieces = lax.all_to_all(pieces, axis, split_axis=0, concat_axis=0)
+    return jnp.concatenate(pieces, axis=join)
 
 
 def passed_along(value, axis, steps):
@@ -168,7 +175,7 @@
 
     attn_grad = jnp.dot(grad_low, all_out, preferred_element_type=jnp.float32).astype(jnp.bfloat16)
     pieces = jnp.stack(project_local(normed_fwd) + project_local(normed_bwd) + [attn_grad])
-    head_view = lax.all_to_all(pieces, "seq", split_axis=2, concat_axis=1, tiled=True)
+    head_view = stacked_exchange(pieces, "seq", 2, 1)
     attn = attend(head_view[0], head_view[1], head_view[2])
     attn_tokens = to_tokens(attn[None])[0]
     branch = times_t(attn_tokens, all_out)

time: 777 us -> 780 us (level)
  local copies, waits for them, and re-layouts: 95 us -> 106 us
    unnamed x32 -> x39, local copies, waits for them, and re-layouts: 14 us -> 26.7 us
where the time goes in v1:
time: 780 us; the launch traced here: 768 us
  waiting for transfers between devices  485 us (62%)
  matrix products  112 us (14%)
  local copies, waits for them, and re-layouts  106 us (14%)
  other arithmetic  29.8 us (4%)
  starting transfers between devices  21.8 us (3%)
  between operations  14.2 us (2%)
    all_gather x1, waiting for transfers between devices, shards(): lax.all_gather(w_key[0], 'seq', axis=1, tiled=True)  118 us
    all_gather x1, waiting for transfers between devices, shards(): lax.all_gather(w_out[0], 'seq', axis=1, tiled=True)  111 us
    all_gather x1, waiting for transfers between devices, shards(): lax.all_gather(w_query[0], 'seq', axis=1, tiled=True)  108 us
    all_gather x1, waiting for transfers between devices, shards(): lax.all_gather(w_value[0], 'seq', axis=1, tiled=True)  80 us
    all_to_all x1, waiting for transfers between devices, stacked_exchange(): pieces = lax.all_to_all(pieces, axis, split_axis=0, concat_axis=0)  49.6 us
    unnamed x39, local copies, waits for them, and re-layouts  26.7 us
    dot_general x4, matrix products, times_t(): lax.dot_general(left, right, (((1,), (1,)), ((), ())), preferred_element_...  23.3 us
  transfers between devices with their start and end apart: 9, of which 7 were waited for; matrix products, arithmetic and copies ran while one was open for 17% of the time, Pallas kernels for 0%

profile of v1, /device:TPU:1, one launch (start us, length us, event | category | flops | bytes accessed | tf_op | source)
XLA Modules:
  0.0 768.0 jit_solution(2046299653418429706)
XLA Ops:
  13.0 118.5 %all-gather.11.cloned.1.call-done = bf16[1,2048,2048]{2,1,0:T(8,128)(2,1)} async-done(((bf16[1,2048,256]{2,1,0:T(8,128)(2,1)}), bf16[1,2048,2048]{2,1,0:T(8,128)(2,1)}) %all-gather.11.cloned.1.call-update) | async-done | bytes 8388624 | tf_op jit(solution)/shard_map/all_gather | solution.py:158
  131.5 12.4 %copy.79 = bf16[2048,2048]{1,0:T(8,128)(2,1)} copy(bf16[2048,2048]{0,1:T(8,128)(2,1)} %bitcast.235) | data formatting | bytes 16777216 | tf_op jit(solution)/shard_map/dot_general | solution.py:169
  143.8 108.1 %all-gather.9.cloned.1.call-done = bf16[1,2048,2048]{2,1,0:T(8,128)(2,1)} async-done(((bf16[1,2048,256]{2,1,0:T(8,128)(2,1)}), bf16[1,2048,2048]{2,1,0:T(8,128)(2,1)}) %all-gather.9.cloned.1.call-update) | async-done | bytes 8388624 | tf_op jit(solution)/shard_map/all_gather | solution.py:157
  251.9 12.4 %copy.78 = bf16[2048,2048]{1,0:T(8,128)(2,1)} copy(bf16[2048,2048]{0,1:T(8,128)(2,1)} %bitcast.236) | data formatting | bytes 16777216 | tf_op jit(solution)/shard_map/dot_general | solution.py:166
  264.3 6.5 fusion.134
  270.9 2.5 fusion.138
  273.6 2.5 fusion.136
  276.1 2.5 fusion.140
  282.4 2.2 pad_maximum_fusion.1
  284.5 2.1 copy.80
  286.6 2.0 copy.81
  292.4 80.0 %all-gather.13.cloned.1.call-done = bf16[1,2048,2048]{2,1,0:T(8,128)(2,1)} async-done(((bf16[1,2048,256]{2,1,0:T(8,128)(2,1)}), bf16[1,2048,2048]{2,1,0:T(8,128)(2,1)}) %all-gather.13.cloned.1.call-update) | async-done | bytes 8388624 | tf_op jit(solution)/shard_map/all_gather | solution.py:159
  372.5 5.7 fusion.76
  379.8 2.4 fusion.70
  382.2 110.6 %all-gather.15.cloned.1.call-done = bf16[1,2048,2048]{2,1,0:T(8,128)(2,1)} async-done(((bf16[1,2048,256]{2,1,0:T(8,128)(2,1)}), bf16[1,2048,2048]{2,1,0:T(8,128)(2,1)}) %all-gather.15.cloned.1.call-update) | async-done | bytes 8388624 | tf_op jit(solution)/shard_map/all_gather | solution.py:160
  492.8 5.5 fusion.64
  512.8 4.5 all-to-all-start
  519.1 49.6 %all-to-all-done = bf16[8,7,128,256]{3,2,1,0:T(8,128)(2,1)} async-done(((bf16[8,7,128,256]{3,2,1,0:T(8,128)(2,1)}), bf16[8,7,128,256]{3,2,1,0:T(8,128)(2,1)}, u32[]{:S(2)}, u32[]{:S(2)}) %all-to-all-start) | async-done | bytes 3670048 | tf_op jit(solution)/shard_map/all_to_all | solution.py:12
  568.7 3.9 fusion.143
  586.4 5.7 fusion.102
  592.1 7.2 fusion.154
  599.3 5.9 fusion.86
  605.2 14.8 %fusion.82 = f32[1024,2,128]{0,2,1:T(8,128)} fusion(bf16[1024,2,128]{0,2,1:T(8,128)(2,1)} %copy.96, f32[2,1024,1024]{1,2,0:T(8,128)} %fusion.102, f32[2,1024,1024]{1,2,0:T(8,128)} %get-tuple-element.78, f32[2,1024]{1,0:T(2,128)S(1)} %get-tuple-element.77), kind=kOutput, calls=%fused_computation.51 | convolution fusion | flops 551554048 | bytes 18358272 | tf_op jit(solution)/shard_map/while/body/eval_jaxpr/hqk,qhd->khd/dot_general | solution.py:125
  619.9 14.6 %fusion.79 = f32[1024,2,128]{0,2,1:T(8,128)} fusion(bf16[1024,2,128]{0,2,1:T(8,128)(2,1)} %copy.94, f32[2,1024,1024]{1,2,0:T(8,128)} %fusion.102, f32[2,1024,1024]{1,2,0:T(8,128)} %get-tuple-element.78, f32[2,1024]{1,0:T(2,128)S(1)} %get-tuple-element.77), kind=kOutput, calls=%fused_computation.50 | convolution fusion | flops 551554048 | bytes 18358272 | tf_op jit(solution)/shard_map/while/body/eval_jaxpr/hqk,khd->qhd/dot_general | solution.py:122
  640.5 7.5 fusion.145
  648.0 5.2 fusion.85
  653.2 3.6 copy.88
  657.3 5.6 reduce
  664.9 4.1 all-to-all-start.1
  669.1 2.7 add_convert_fusion.1
  672.6 3.6 copy.102
  676.2 3.6 copy.100
  681.6 3.6 copy.101
  685.2 6.0 pad_maximum_fusion
  691.1 6.5 all-to-all-start.2
  697.7 3.5 reshape.327
  701.1 2.1 copy.111
  703.2 2.0 copy.89
  705.3 7.3 fusion.58
  712.6 4.0 collective-permute-start
  716.5 9.9 %all-to-all-done.2 = bf16[3,1024,256]{2,0,1:T(4,128)(2,1)} async-done(((bf16[3,1024,256]{2,0,1:T(4,128)(2,1)}), bf16[3,1024,256]{2,0,1:T(4,128)(2,1)}, u32[]{:S(2)}, u32[]{:S(2)}) %all-to-all-start.2) | async-done | bytes 1572896 | tf_op jit(solution)/shard_map/all_to_all | solution.py:142
  729.2 2.1 copy.106
  733.3 6.6 fusion.13
  739.9 6.5 fusion.37
  746.4 3.0 fusion.91
  749.8 2.5 collective-permute-start.1
  752.2 2.1 bitcast_convert_fusion.3
  754.3 5.9 collective-permute-done.1
  (82 shorter events, 62.8 us)
Async XLA Ops:
  7.2 124.3 %all-gather.11.cloned.1.call-start = ((), (), s32[]{:S(2)}) async-start(), calls=%async_computation.4 | async-start | bytes 9437184 | tf_op jit(solution)/shard_map/all_gather | solution.py:158
  7.9 244.0 %all-gather.9.cloned.1.call-start = ((), (), s32[]{:S(2)}) async-start(), calls=%async_computation.3 | async-start | bytes 9437184 | tf_op jit(solution)/shard_map/all_gather | solution.py:157
  8.6 363.8 %all-gather.13.cloned.1.call-start = ((), (), s32[]{:S(2)}) async-start(), calls=%async_computation.5 | async-start | bytes 9437184 | tf_op jit(solution)/shard_map/all_gather | solution.py:159
  9.4 483.4 %all-gather.15.cloned.1.call-start = ((), (), s32[]{:S(2)}) async-start(), calls=%async_computation.6 | async-start | bytes 9437184 | tf_op jit(solution)/shard_map/all_gather | solution.py:160
  251.9 12.4 %copy-start.2 = (f32[1,128,2048]{2,1,0:T(8,128)S(1)}, f32[1,128,2048]{2,1,0:T(8,128)}, u32[]{:S(2)}) copy-start(f32[1,128,2048]{2,1,0:T(8,128)} %param.9) | copy-start | bytes 3145732
  251.9 12.4 %copy-start.7 = (f32[1,2048]{1,0:T(1,128)S(1)}, f32[1,2048]{1,0:T(1,128)}, u32[]{:S(2)}) copy-start(f32[1,2048]{1,0:T(1,128)} %param.11) | copy-start | bytes 24580
  264.3 6.5 copy-start.1
  264.3 6.6 copy-start.3
  264.3 9.1 %slice-start.2 = ((s8[8388608]{0:T(1024)(128)(4,1)}), s8[4194304]{0:T(1024)(128)(4,1)S(1)}, s32[]{:S(2)}) async-start(s8[8388608]{0:T(1024)(128)(4,1)} %bitcast.231), calls=%async_computation.9 | async-start | bytes 8388608
  270.9 2.7 slice-start.3
  372.5 7.3 copy-start
  379.8 113.0 %copy-start.4 = (f32[1,128,2048]{2,1,0:T(8,128)S(1)}, f32[1,128,2048]{2,1,0:T(8,128)}, u32[]{:S(2)}) copy-start(f32[1,128,2048]{2,1,0:T(8,128)} %param.10) | copy-start | bytes 3145732
  512.8 55.9 %all-to-all-start = ((bf16[8,7,128,256]{3,2,1,0:T(8,128)(2,1)}), bf16[8,7,128,256]{3,2,1,0:T(8,128)(2,1)}, u32[]{:S(2)}, u32[]{:S(2)}) async-start(bf16[8,7,128,256]{3,2,1,0:T(8,128)(2,1)} %fusion.120), calls=%async_computation | async-start | bytes 7340032 | tf_op jit(solution)/shard_map/all_to_all | solution.py:12
  664.9 26.2 %all-to-all-start.1 = ((bf16[8,2,16384]{2,1,0:T(2,128)(2,1)}), bf16[8,2,16384]{2,1,0:T(2,128)(2,1)}, u32[]{:S(2)}, u32[]{:S(2)}) async-start(bf16[8,2,16384]{2,1,0:T(2,128)(2,1)} %reshape.326), calls=%async_computation.1 | async-start | bytes 1048576 | tf_op jit(solution)/shard_map/all_to_all | solution.py:142
  691.1 35.3 %all-to-all-start.2 = ((bf16[3,1024,256]{2,0,1:T(4,128)(2,1)}), bf16[3,1024,256]{2,0,1:T(4,128)(2,1)}, u32[]{:S(2)}, u32[]{:S(2)}) async-start(bf16[3,1024,256]{2,0,1:T(4,128)(2,1)} %pad_maximum_fusion), calls=%async_computation.2 | async-start | bytes 4194304 | tf_op jit(solution)/shard_map/all_to_all | solution.py:142
  712.6 39.7 %collective-permute-start = (bf16[128,2048]{1,0:T(8,128)(2,1)}, bf16[128,2048]{1,0:T(8,128)(2,1)}, u32[]{:S(2)}, u32[]{:S(2)}) collective-permute-start(bf16[128,2048]{1,0:T(8,128)(2,1)} %fusion.58), channel_id=1, source_target_pairs={{0,8},{8,16},{16,24},{24,32},{32,40},{40,48},{48,56},{56,64},{64,7... | collective-permute-start | bytes 1572872 | tf_op jit(solution)/shard_map/ppermute | solution.py:19
  733.3 6.6 copy-start.6
  733.3 13.1 %slice-start = ((s8[8388608]{0:T(1024)(128)(4,1)}), s8[4194304]{0:T(1024)(128)(4,1)S(1)}, s32[]{:S(2)}) async-start(s8[8388608]{0:T(1024)(128)(4,1)} %bitcast.227), calls=%async_computation.7 | async-start | bytes 8388608
  733.3 13.1 %copy-start.5 = (bf16[1,128,8,256]{1,3,2,0:T(8,128)(2,1)S(1)}, bf16[1,128,8,256]{1,3,2,0:T(8,128)(2,1)}, u32[]{:S(2)}) copy-start(bf16[1,128,8,256]{1,3,2,0:T(8,128)(2,1)} %copy.106) | copy-start | bytes 1572868
  739.9 6.5 slice-start.1
  749.8 10.5 %collective-permute-start.1 = (bf16[128,2048]{1,0:T(8,128)(2,1)S(1)}, bf16[128,2048]{1,0:T(8,128)(2,1)S(1)}, u32[]{:S(2)}, u32[]{:S(2)}) collective-permute-start(bf16[128,2048]{1,0:T(8,128)(2,1)S(1)} %fusion.89), channel_id=1, source_target_pairs={{0,120},{8,0},{16,8},{24,16},{32,24},{40,32},{48,40},{56,48},{64,5... | collective-permute-start | bytes 1572872 | tf_op jit(solution)/shard_map/ppermute | solution.py:19
Sparse Core Ops, SparseCore 0:
  10.2 121.2 all-gather.10
  133.6 118.2 all-gather.8
  254.1 118.3 all-gather.12
  374.5 118.2 all-gather.14
